TPU v7x, 128 devices: a whole 4x4x4 slice. The times are simulated.
128 devices in a mesh: mp: 8 (over x, z_lo), item: 16 (over z_hi, y, core).
Axes of the slice: x: 4, y: 4, z: 4 (z_hi: 2, z_lo: 2; z = z_hi * 2 + z_lo), core: 2. Of those that a mesh axis runs over, the one named last changes fastest.
Arguments:
- response: int32 [16384, 32768], P('mp', 'item'), may hold values from 0 to 2
- difficulty: float32 [32768], P('item'), may hold values from -4 to 4
- ability: float32 [16384, 256], P('mp', 'item'), may hold values from -6 to 6
- ability_m: float32 [16384, 256], P('mp', 'item'), may hold values from -3 to 3
- ability_v: float32 [16384, 256], P('mp', 'item'), may hold values from 0.02 to 0.5
- discrim: float32 [32768, 256], P('item', 'mp'), may hold values from -0.375 to 0.375
- discrim_m: float32 [32768, 256], P('item', 'mp'), may hold values from -3 to 3
- discrim_v: float32 [32768, 256], P('item', 'mp'), may hold values from 0.02 to 0.5
Outputs:
- ability_new: float32 [16384, 256], P('mp', 'item')
- ability_m_new: float32 [16384, 256], P('mp', 'item')
- ability_v_new: float32 [16384, 256], P('mp', 'item')
- discrim_new: float32 [32768, 256], P('item', 'mp')
- discrim_m_new: float32 [32768, 256], P('item', 'mp')
- discrim_v_new: float32 [32768, 256], P('item', 'mp')
Inputs may be any that keep to these rules, and one draw needn't show every extreme that they name: `response`: 0 marks an unobserved pair, 1 an observed wrong answer, 2 an observed right answer.
All inputs are finite; a program needn't handle non-finite values.
Results may differ from a plain program's by a relative error of at most 0.0012.
Values may be sent and summed in bfloat16 or wider, within the bound.
A program may use at most 128 MiB of HBM per device.

v0:
```python
import math
import jax
import jax.numpy as jnp
from jax import lax
from jax.sharding import PartitionSpec as P

K = 256
beta_one = 0.9
beta_two = 0.999
corr_one = 1.0 - 0.9**10
corr_two = 1.0 - 0.999**10
adam_eps = 1e-08


def adam_update(factor, moment, second, gradient, step_rate):
    moment_new = beta_one * moment + (1.0 - beta_one) * gradient
    second_new = beta_two * second + (1.0 - beta_two) * gradient * gradient
    update = moment_new / corr_one / (jnp.sqrt(second_new / corr_two) + adam_eps)
    return (factor - step_rate * update, moment_new, second_new)


def shards(response, difficulty, ability, ability_m, ability_v, discrim, discrim_m, discrim_v):
    ability_full = lax.all_gather(ability.astype(jnp.bfloat16), "item", axis=1, tiled=True)
    discrim_full = lax.all_gather(discrim.astype(jnp.bfloat16), "mp", axis=1, tiled=True)
    logits = lax.dot_general(
        ability_full, discrim_full, (((1,), (1,)), ((), ())), preferred_element_type=jnp.float32
    )
    logits = logits + difficulty[None, :]
    correct = (response == 2).astype(jnp.float32)
    residual = jnp.where(response > 0, jax.nn.sigmoid(logits) - correct, jnp.float32(0.0))
    ability_wide = ability_full.astype(jnp.float32)
    discrim_wide = discrim_full.astype(jnp.float32)
    highest = lax.Precision.HIGHEST
    ability_cols = ability.shape[1]
    discrim_cols = discrim.shape[1]
    items_total = response.shape[1] * lax.axis_size("item")
    ckpts_total = response.shape[0] * lax.axis_size("mp")
    ability_partial = jnp.dot(residual, discrim_wide, precision=highest)
    ability_sum = lax.psum(ability_partial, "item")
    ability_grad = lax.dynamic_slice_in_dim(
        ability_sum, lax.axis_index("item") * ability_cols, ability_cols, 1
    )
    discrim_partial = lax.dot_general(
        residual, ability_wide, (((0,), (0,)), ((), ())), precision=highest
    )
    discrim_sum = lax.psum(discrim_partial, "mp")
    discrim_grad = lax.dynamic_slice_in_dim(
        discrim_sum, lax.axis_index("mp") * discrim_cols, discrim_cols, 1
    )
    ability_grad = ability_grad * math.sqrt(K / items_total)
    discrim_grad = discrim_grad * math.sqrt(1.0 / ckpts_total)
    ability_new, ability_m_new, ability_v_new = adam_update(
        ability, ability_m, ability_v, ability_grad, 0.05
    )
    discrim_new, discrim_m_new, discrim_v_new = adam_update(
        discrim, discrim_m, discrim_v, discrim_grad, 0.01
    )
    return (ability_new, ability_m_new, ability_v_new, discrim_new, discrim_m_new, discrim_v_new)


def solution(mesh):
    return jax.shard_map(
        shards,
        mesh=mesh,
        in_specs=(
            P("mp", "item"),
            P("item"),
            P("mp", "item"),
            P("mp", "item"),
            P("mp", "item"),
            P("item", "mp"),
            P("item", "mp"),
            P("item", "mp"),
        ),
        out_specs=(
            P("mp", "item"),
            P("mp", "item"),
            P("mp", "item"),
            P("item", "mp"),
            P("item", "mp"),
            P("item", "mp"),
        ),
        check_vma=False,
    )
```

profile of v0, /device:TPU:8, one launch (start us, length us, event | category | flops | bytes accessed | tf_op | source)
XLA Modules:
  0.0 386.6 jit_solution(2040958627910483739)
XLA Ops:
  7.2 0.0 all-gather.5.cloned.1.call-start
  7.2 1.6 convert_element_type.12
  8.8 0.0 all-gather.5.cloned.1.call-update
  8.9 0.0 all-gather.3.cloned.1.call-start
  8.9 1.5 convert_element_type.11
  10.5 0.0 all-gather.3.cloned.1.call-update
  10.5 0.0 all-reduce.3.cloned.1.call-start
  10.5 40.9 %all-gather.5.cloned.1.call-done = bf16[2048,256]{0,1:T(8,128)(2,1)} async-done(((bf16[2048,32]{0,1:T(8,128)(2,1)}), bf16[2048,256]{0,1:T(8,128)(2,1)}) %all-gather.5.cloned.1.call-update) | async-done | bytes 1048592 | tf_op jit(solution)/shard_map/all_gather | solution.py:24
  51.5 0.0 copy-start.2
  51.5 47.4 %all-gather.3.cloned.1.call-done = bf16[2048,256]{0,1:T(8,128)(2,1)} async-done(((bf16[2048,16]{0,1:T(8,128)(2,1)}), bf16[2048,256]{0,1:T(8,128)(2,1)}) %all-gather.3.cloned.1.call-update) | async-done | bytes 1048592 | tf_op jit(solution)/shard_map/all_gather | solution.py:23
  98.8 12.2 %subtract_select_fusion = f32[2048,2048]{1,0:T(8,128)S(1)} fusion(s32[2048,2048]{1,0:T(8,128)} %param.8, bf16[2048,256]{0,1:T(8,128)(2,1)} %all-gather.3.cloned.1.call-done, bf16[2048,256]{0,1:T(8,128)(2,1)} %all-gather.5.cloned.1.call-done, f32[2048]{0:T(1024)} %param.9), kind=kOutput, calls=%fused_computation | convolution fusion | flops 2185232384 | bytes 35659776 | tf_op jit(solution)/shard_map/dot_general | solution.py:25
  111.0 0.0 copy-start
  111.0 5.7 %copy-done = f32[2048,2048]{1,0:T(8,128)} copy-done((f32[2048,2048]{1,0:T(8,128)}, f32[2048,2048]{1,0:T(8,128)S(1)}, u32[]{:S(2)}) %copy-start) | copy-done | bytes 16777240
  116.7 0.0 copy-done.2
  116.7 0.0 copy-start.1
  116.7 9.8 %fusion = f32[2048,256]{0,1:T(8,128)} fusion(f32[2048,2048]{1,0:T(8,128)S(1)} %subtract_select_fusion, bf16[2048,256]{0,1:T(8,128)(2,1)S(1)} %copy-done.2), kind=kOutput, calls=%fused_computation.7 | convolution fusion | flops 12884901888 | bytes 19922944 | tf_op jit(solution)/shard_map/dot_general | solution.py:38
  126.5 0.0 copy-start.4
  126.5 0.0 copy-start.7
  126.5 0.0 copy-start.8
  126.5 0.0 copy-start.3
  126.5 0.0 copy-start.5
  126.5 0.0 copy-start.6
  126.5 0.0 all-reduce.3.cloned.1.call-update
  126.6 0.2 all-reduce.5.cloned.1.call-start
  126.8 0.0 copy-done.1
  126.8 13.3 %fusion.1 = f32[2048,256]{0,1:T(8,128)} fusion(f32[2048,2048]{1,0:T(8,128)} %copy-done, bf16[2048,256]{0,1:T(8,128)(2,1)S(1)} %copy-done.1), kind=kOutput, calls=%fused_computation.8 | convolution fusion | flops 12884901888 | bytes 19922944 | tf_op jit(solution)/shard_map/dot_general | solution.py:43
  140.1 0.0 all-reduce.5.cloned.1.call-update
  140.1 124.7 %all-reduce.3.cloned.1.call-done = f32[2048,256]{0,1:T(8,128)} async-done(((f32[2048,256]{0,1:T(8,128)}), f32[2048,256]{0,1:T(8,128)}) %all-reduce.3.cloned.1.call-update) | async-done | bytes 2097168 | tf_op jit(solution)/shard_map/psum | solution.py:39
  264.8 0.0 copy-done.4
  264.8 0.0 copy-done.7
  264.8 0.0 copy-done.8
  264.8 1.7 multiply_subtract_fusion.1
  266.5 111.6 %all-reduce.5.cloned.1.call-done = f32[2048,256]{0,1:T(8,128)} async-done(((f32[2048,256]{0,1:T(8,128)}), f32[2048,256]{0,1:T(8,128)}) %all-reduce.5.cloned.1.call-update) | async-done | bytes 2097168 | tf_op jit(solution)/shard_map/psum | solution.py:46
  378.1 0.0 copy-done.3
  378.1 0.0 copy-done.5
  378.1 0.0 copy-done.6
  378.1 1.9 multiply_subtract_fusion
Async XLA Ops:
  7.2 44.3 %all-gather.5.cloned.1.call-start = ((), (), s32[]{:S(2)}) async-start(), calls=%async_computation.1 | async-start | bytes 1179648 | tf_op jit(solution)/shard_map/all_gather | solution.py:24
  8.9 90.0 %all-gather.3.cloned.1.call-start = ((), (), s32[]{:S(2)}) async-start(), calls=%async_computation | async-start | bytes 1114112 | tf_op jit(solution)/shard_map/all_gather | solution.py:23
  10.5 254.3 %all-reduce.3.cloned.1.call-start = ((), (), s32[]{:S(2)}) async-start(), calls=%async_computation.2 | async-start | bytes 4194304 | tf_op jit(solution)/shard_map/psum | solution.py:39
  51.5 65.3 %copy-start.2 = (bf16[2048,256]{0,1:T(8,128)(2,1)S(1)}, bf16[2048,256]{0,1:T(8,128)(2,1)}, u32[]{:S(2)}) copy-start(bf16[2048,256]{0,1:T(8,128)(2,1)} %all-gather.5.cloned.1.call-done) | copy-start | bytes 3145732
  111.0 5.7 %copy-start = (f32[2048,2048]{1,0:T(8,128)}, f32[2048,2048]{1,0:T(8,128)S(1)}, u32[]{:S(2)}) copy-start(f32[2048,2048]{1,0:T(8,128)S(1)} %subtract_select_fusion) | copy-start | bytes 50331652
  116.7 10.1 %copy-start.1 = (bf16[2048,256]{0,1:T(8,128)(2,1)S(1)}, bf16[2048,256]{0,1:T(8,128)(2,1)}, u32[]{:S(2)}) copy-start(bf16[2048,256]{0,1:T(8,128)(2,1)} %all-gather.3.cloned.1.call-done) | copy-start | bytes 3145732
  126.5 138.3 %copy-start.4 = (f32[2048,16]{0,1:T(8,128)S(1)}, f32[2048,16]{0,1:T(8,128)}, u32[]{:S(2)}) copy-start(f32[2048,16]{0,1:T(8,128)} %param.10) | copy-start | bytes 393220
  126.5 138.3 %copy-start.7 = (f32[2048,16]{0,1:T(8,128)S(1)}, f32[2048,16]{0,1:T(8,128)}, u32[]{:S(2)}) copy-start(f32[2048,16]{0,1:T(8,128)} %param.11) | copy-start | bytes 393220
  126.5 138.3 %copy-start.8 = (f32[2048,16]{0,1:T(8,128)S(1)}, f32[2048,16]{0,1:T(8,128)}, u32[]{:S(2)}) copy-start(f32[2048,16]{0,1:T(8,128)} %param.12) | copy-start | bytes 393220
  126.5 251.6 %copy-start.3 = (f32[2048,32]{0,1:T(8,128)S(1)}, f32[2048,32]{0,1:T(8,128)}, u32[]{:S(2)}) copy-start(f32[2048,32]{0,1:T(8,128)} %param.13) | copy-start | bytes 786436
  126.5 251.6 %copy-start.5 = (f32[2048,32]{0,1:T(8,128)S(1)}, f32[2048,32]{0,1:T(8,128)}, u32[]{:S(2)}) copy-start(f32[2048,32]{0,1:T(8,128)} %param.14) | copy-start | bytes 786436
  126.5 251.6 %copy-start.6 = (f32[2048,32]{0,1:T(8,128)S(1)}, f32[2048,32]{0,1:T(8,128)}, u32[]{:S(2)}) copy-start(f32[2048,32]{0,1:T(8,128)} %param.15) | copy-start | bytes 786436
  126.6 251.6 %all-reduce.5.cloned.1.call-start = ((), (), s32[]{:S(2)}) async-start(), calls=%async_computation.3 | async-start | bytes 4194304 | tf_op jit(solution)/shard_map/psum | solution.py:46
Sparse Core Ops, SparseCore 0:
  10.2 41.2 all-gather.4
  54.5 44.3 all-gather.2
  126.7 138.0 all-reduce.2
  267.2 110.9 all-reduce.4
where the time goes:
time: 387 us
  waiting for transfers between devices  325 us (84%)
  matrix products  35.2 us (9%)
  between operations  13.8 us (4%)
  other arithmetic  6.8 us (2%)
  local copies, waits for them, and re-layouts  5.78 us (1%)
    psum x1, waiting for transfers between devices, shards(): ability_sum = lax.psum(ability_partial, 'item')  125 us
    psum x1, waiting for transfers between devices, shards(): discrim_sum = lax.psum(discrim_partial, 'mp')  112 us
    all_gather x1, waiting for transfers between devices, shards(): lax.all_gather(ability.astype(jnp.bfloat16), 'item', axis=1, tiled=True)  47.4 us
    all_gather x1, waiting for transfers between devices, shards(): lax.all_gather(discrim.astype(jnp.bfloat16), 'mp', axis=1, tiled=True)  40.9 us
    dot_general x1, matrix products, shards(): lax.dot_general(residual, ability_wide, (((0,), (0,)), ((), ())), precisi...  13.3 us
    dot_general x1, matrix products, shards(): lax.dot_general(ability_full, discrim_full, (((1,), (1,)), ((), ())), pre...  12.2 us
    dot_general x1, matrix products, shards(): ability_partial = jnp.dot(residual, discrim_wide, precision=highest)  9.76 us
  transfers between devices with their start and end apart: 4, of which 4 were waited for; matrix products, arithmetic and copies ran while one was open for 4% of the time, Pallas kernels for 0%

commit v1 on v0

--- a/solution.py
+++ b/solution.py
@@ -12,6 +12,13 @@
 adam_eps = 1e-08
 
 
+def swapped_in(block, name, along):
+    n_dev = lax.axis_size(name)
+    pieces = jnp.stack([block for _ in range(n_dev)])
+    pieces = lax.all_to_all(pieces, name, split_axis=0, concat_axis=0)
+    return jnp.concatenate(pieces, axis=along)
+
+
 def adam_update(factor, moment, second, gradient, step_rate):
     moment_new = beta_one * moment + (1.0 - beta_one) * gradient
     second_new = beta_two * second + (1.0 - beta_two) * gradient * gradient
@@ -20,7 +27,7 @@
 
 
 def shards(response, difficulty, ability, ability_m, ability_v, discrim, discrim_m, discrim_v):
-    ability_full = lax.all_gather(ability.astype(jnp.bfloat16), "item", axis=1, tiled=True)
+    ability_full = swapped_in(ability.astype(jnp.bfloat16), "item", 1)
     discrim_full = lax.all_gather(discrim.astype(jnp.bfloat16), "mp", axis=1, tiled=True)
     logits = lax.dot_general(
         ability_full, discrim_full, (((1,), (1,)), ((), ())), preferred_element_type=jnp.float32

time: 387 us -> 347 us (0.90)
  waiting for transfers between devices: 325 us -> 260 us
  blocking collectives: 0 us -> 26.3 us
    all_gather x1 -> x0, waiting for transfers between devices: 47.4 us -> none  [shards(): lax.all_gather(ability.astype(jnp.bfloat16), 'item', axis=1, tiled=True)]
    all_to_all x0 -> x1, blocking collectives: none -> 26.3 us  [swapped_in(): pieces = lax.all_to_all(pieces, name, split_axis=0, concat_axis=0)]
    all_gather x1, waiting for transfers between devices: 40.9 us -> 21.6 us  [shards(): lax.all_gather(discrim.astype(jnp.bfloat16), 'mp', axis=1, tiled=True)]
  transfers between devices with their start and end apart: 4 -> 3, of which waited for: 4 -> 3; matrix products, arithmetic and copies ran while one was open for 4% -> 5% of each run, Pallas kernels for 0% -> 0%
where the time goes in v1:
time: 347 us
  waiting for transfers between devices  260 us (75%)
  matrix products  34.9 us (10%)
  blocking collectives  26.3 us (8%)
  between operations  13.8 us (4%)
  other arithmetic  6.17 us (2%)
  local copies, waits for them, and re-layouts  5.86 us (2%)
    psum x1, waiting for transfers between devices, shards(): ability_sum = lax.psum(ability_partial, 'item')  126 us
    psum x1, waiting for transfers between devices, shards(): discrim_sum = lax.psum(discrim_partial, 'mp')  112 us
    all_to_all x1, blocking collectives, swapped_in(): pieces = lax.all_to_all(pieces, name, split_axis=0, concat_axis=0)  26.3 us
    all_gather x1, waiting for transfers between devices, shards(): lax.all_gather(discrim.astype(jnp.bfloat16), 'mp', axis=1, tiled=True)  21.6 us
    dot_general x1, matrix products, shards(): lax.dot_general(residual, ability_wide, (((0,), (0,)), ((), ())), precisi...  13.3 us
    dot_general x1, matrix products, shards(): lax.dot_general(ability_full, discrim_full, (((1,), (1,)), ((), ())), pre...  11.9 us
    dot_general x1, matrix products, shards(): ability_partial = jnp.dot(residual, discrim_wide, precision=highest)  9.74 us
  transfers between devices with their start and end apart: 3, of which 3 were waited for; matrix products, arithmetic and copies ran while one was open for 5% of the time, Pallas kernels for 0%

profile of v1, /device:TPU:8, one launch (start us, length us, event | category | flops | bytes accessed | tf_op | source)
XLA Modules:
  0.0 347.2 jit_solution(16482083117351154533)
XLA Ops:
  7.2 0.0 all-gather.2.cloned.1.call-start
  7.2 1.6 convert_element_type.12
  8.8 0.0 all-gather.2.cloned.1.call-update
  8.9 0.0 all-reduce.3.cloned.1.call-start
  8.9 0.9 convert_element_type.11
  9.8 0.1 stack.2
  9.9 26.3 %all_to_all.5 = bf16[16,2048,16]{1,2,0:T(8,128)(2,1)S(1)} all-to-all(bf16[16,2048,16]{1,2,0:T(8,128)(2,1)S(1)} %stack.2), channel_id=1, replica_groups=mesh['mp'=8,'item'=16] {'item'}, dimensions={0} | all-to-all | bytes 2097152 | tf_op jit(solution)/shard_map/all_to_all | solution.py:18
  36.2 21.6 %all-gather.2.cloned.1.call-done = bf16[2048,256]{0,1:T(8,128)(2,1)} async-done(((bf16[2048,32]{0,1:T(8,128)(2,1)}), bf16[2048,256]{0,1:T(8,128)(2,1)}) %all-gather.2.cloned.1.call-update) | async-done | bytes 1048592 | tf_op jit(solution)/shard_map/all_gather | solution.py:31
  57.8 0.0 copy-start.1
  57.8 11.9 %subtract_select_fusion = f32[2048,2048]{1,0:T(8,128)S(1)} fusion(s32[2048,2048]{1,0:T(8,128)} %param.8, bf16[2048,256]{0,1:T(8,128)(2,1)S(1)} %bitcast.9, bf16[2048,256]{0,1:T(8,128)(2,1)} %all-gather.2.cloned.1.call-done, f32[2048]{0:T(1024)} %param.9), kind=kOutput, calls=%fused_computation | convolution fusion | flops 2185232384 | bytes 35659776 | tf_op jit(solution)/shard_map/dot_general | solution.py:32
  69.7 0.0 copy-start
  69.7 5.7 %copy-done = f32[2048,2048]{1,0:T(8,128)} copy-done((f32[2048,2048]{1,0:T(8,128)}, f32[2048,2048]{1,0:T(8,128)S(1)}, u32[]{:S(2)}) %copy-start) | copy-done | bytes 16777240
  75.4 0.0 copy-done.1
  75.4 9.7 %fusion = f32[2048,256]{0,1:T(8,128)} fusion(f32[2048,2048]{1,0:T(8,128)S(1)} %subtract_select_fusion, bf16[2048,256]{0,1:T(8,128)(2,1)S(1)} %copy-done.1), kind=kOutput, calls=%fused_computation.7 | convolution fusion | flops 12884901888 | bytes 19922944 | tf_op jit(solution)/shard_map/dot_general | solution.py:45
  85.2 0.0 copy-start.3
  85.2 0.0 copy-start.6
  85.2 0.0 copy-start.7
  85.2 0.0 copy-start.2
  85.2 0.0 copy-start.4
  85.2 0.0 copy-start.5
  85.2 0.0 all-reduce.3.cloned.1.call-update
  85.2 0.2 all-reduce.5.cloned.1.call-start
  85.5 13.3 %fusion.1 = f32[2048,256]{0,1:T(8,128)} fusion(f32[2048,2048]{1,0:T(8,128)} %copy-done, bf16[2048,256]{0,1:T(8,128)(2,1)S(1)} %bitcast.10), kind=kOutput, calls=%fused_computation.8 | convolution fusion | flops 12884901888 | bytes 19922944 | tf_op jit(solution)/shard_map/dot_general | solution.py:50
  98.8 0.0 all-reduce.5.cloned.1.call-update
  98.8 126.5 %all-reduce.3.cloned.1.call-done = f32[2048,256]{0,1:T(8,128)} async-done(((f32[2048,256]{0,1:T(8,128)}), f32[2048,256]{0,1:T(8,128)}) %all-reduce.3.cloned.1.call-update) | async-done | bytes 2097168 | tf_op jit(solution)/shard_map/psum | solution.py:46
  225.3 0.0 copy-done.3
  225.3 0.0 copy-done.6
  225.3 0.0 copy-done.7
  225.3 1.7 multiply_subtract_fusion.1
  227.0 111.8 %all-reduce.5.cloned.1.call-done = f32[2048,256]{0,1:T(8,128)} async-done(((f32[2048,256]{0,1:T(8,128)}), f32[2048,256]{0,1:T(8,128)}) %all-reduce.5.cloned.1.call-update) | async-done | bytes 2097168 | tf_op jit(solution)/shard_map/psum | solution.py:53
  338.8 0.0 copy-done.2
  338.8 0.0 copy-done.4
  338.8 0.0 copy-done.5
  338.8 1.9 multiply_subtract_fusion
Async XLA Ops:
  7.2 50.6 %all-gather.2.cloned.1.call-start = ((), (), s32[]{:S(2)}) async-start(), calls=%async_computation.1 | async-start | bytes 1179648 | tf_op jit(solution)/shard_map/all_gather | solution.py:31
  8.9 216.4 %all-reduce.3.cloned.1.call-start = ((), (), s32[]{:S(2)}) async-start(), calls=%async_computation.2 | async-start | bytes 4194304 | tf_op jit(solution)/shard_map/psum | solution.py:46
  57.8 17.6 %copy-start.1 = (bf16[2048,256]{0,1:T(8,128)(2,1)S(1)}, bf16[2048,256]{0,1:T(8,128)(2,1)}, u32[]{:S(2)}) copy-start(bf16[2048,256]{0,1:T(8,128)(2,1)} %all-gather.2.cloned.1.call-done) | copy-start | bytes 3145732
  69.7 5.7 %copy-start = (f32[2048,2048]{1,0:T(8,128)}, f32[2048,2048]{1,0:T(8,128)S(1)}, u32[]{:S(2)}) copy-start(f32[2048,2048]{1,0:T(8,128)S(1)} %subtract_select_fusion) | copy-start | bytes 50331652
  85.2 140.1 %copy-start.3 = (f32[2048,16]{0,1:T(8,128)S(1)}, f32[2048,16]{0,1:T(8,128)}, u32[]{:S(2)}) copy-start(f32[2048,16]{0,1:T(8,128)} %param.10) | copy-start | bytes 393220
  85.2 140.1 %copy-start.6 = (f32[2048,16]{0,1:T(8,128)S(1)}, f32[2048,16]{0,1:T(8,128)}, u32[]{:S(2)}) copy-start(f32[2048,16]{0,1:T(8,128)} %param.11) | copy-start | bytes 393220
  85.2 140.1 %copy-start.7 = (f32[2048,16]{0,1:T(8,128)S(1)}, f32[2048,16]{0,1:T(8,128)}, u32[]{:S(2)}) copy-start(f32[2048,16]{0,1:T(8,128)} %param.12) | copy-start | bytes 393220
  85.2 253.6 %copy-start.2 = (f32[2048,32]{0,1:T(8,128)S(1)}, f32[2048,32]{0,1:T(8,128)}, u32[]{:S(2)}) copy-start(f32[2048,32]{0,1:T(8,128)} %param.13) | copy-start | bytes 786436
  85.2 253.6 %copy-start.4 = (f32[2048,32]{0,1:T(8,128)S(1)}, f32[2048,32]{0,1:T(8,128)}, u32[]{:S(2)}) copy-start(f32[2048,32]{0,1:T(8,128)} %param.14) | copy-start | bytes 786436
  85.2 253.6 %copy-start.5 = (f32[2048,32]{0,1:T(8,128)S(1)}, f32[2048,32]{0,1:T(8,128)}, u32[]{:S(2)}) copy-start(f32[2048,32]{0,1:T(8,128)} %param.15) | copy-start | bytes 786436
  85.2 253.5 %all-reduce.5.cloned.1.call-start = ((), (), s32[]{:S(2)}) async-start(), calls=%async_computation.3 | async-start | bytes 4194304 | tf_op jit(solution)/shard_map/psum | solution.py:53
Sparse Core Ops, SparseCore 0:
  10.2 47.5 all-gather.1
  85.4 139.8 all-reduce.2
  227.8 110.9 all-reduce.4
